TPU v7x, 32 devices: a whole 2x2x4 slice. The times are simulated.
32 devices in a mesh: grp: 2 (over y), row: 4 (over z), col: 2 (over x), rep: 2 (over core).
Axes of the slice: x: 2, y: 2, z: 4, core: 2. Of those that a mesh axis runs over, the one named last changes fastest.
Arguments:
- emb_row: bfloat16 [2048, 1280], P(('grp', 'row', 'rep'), 'col'), parts along dimension 0, may hold values from -6 to 6
- emb_col: bfloat16 [512, 1280], P(('grp', 'col'), 'row'), parts along dimension 0, may hold values from -6 to 6
- proj_row: bfloat16 [1280, 64], replicated, may hold values from -0.15625 to 0.15625
- proj_col: bfloat16 [1280, 64], replicated, may hold values from -0.15625 to 0.15625
- pair_out: bfloat16 [64, 64], replicated, may hold values from -0.75 to 0.75
- pair_bias: float32 [64], replicated, may hold values from -3 to 3
- conv_weight: bfloat16 [3, 3, 64, 64], replicated, may hold values from -0.25 to 0.25
- conv_bias: float32 [64], replicated, may hold values from -3 to 3
- target: bfloat16 [64, 2048, 256], P(None, ('grp', 'row', 'rep'), 'col'), parts along dimension 1, may hold values from -6 to 6
- kept_tiles: int32 [16, 2], P(('grp', 'row', 'rep'), 'col'), parts along dimension 0, may hold values 0 or 1
Outputs:
- cell_loss: float32 [2048, 256], P(('grp', 'row', 'rep'), 'col'), parts along dimension 0
- grad_conv: float32 [6, 3, 64, 64], P('grp'), parts along dimension 0
- grad_bias: float32 [128], P('grp'), parts along dimension 0
There are 2 independent parts, one for each index of `grp`. A program takes and returns all parts, laid end to end along the dimension named above; an argument that names none is the same for every part. Nothing has to cross between parts.
All inputs are finite; a program needn't handle non-finite values. No bound on the sum of `kept_tiles` on one device may be relied on, other than what follows from the above.
Results may differ from a plain program's by a relative error of at most 0.0025.
Values may be sent and summed in bfloat16 or wider, within the bound.
A program may use at most 128 MiB of HBM per device.

v0:
```python
import functools

import jax
import jax.numpy as jnp
from jax import lax
from jax.experimental import pallas as pl
from jax.experimental.pallas import tpu as pltpu
from jax.sharding import PartitionSpec as P

MESH = pl.DeviceIdType.MESH
F32 = jnp.float32
BF16 = jnp.bfloat16
NT = (((1,), (1,)), ((), ()))


def loop(low, high, body):
    if high - low <= 16:
        for d in range(low, high):
            body(d)
    else:
        lax.fori_loop(low, high, lambda d, _: (body(d), 0)[1], 0)


def kernel(
    sizes,
    emb_row,
    emb_col,
    proj_row,
    proj_col,
    pair_out,
    pair_bias,
    conv_weight,
    conv_bias,
    target,
    kept,
    loss_out,
    conv_grad_out,
    bias_out,
    rowbuf,
    rowedge,
    colbuf,
    coledge,
    row_feat,
    col_wide,
    wide_t,
    target32,
    hid,
    base,
    grad_in,
    weight_f,
    total,
    bias_acc,
    part,
    reduced,
    full,
    row_send,
    row_recv,
    redge_send,
    redge_recv,
    col_send,
    col_recv,
    cedge_send,
    cedge_recv,
    rs_send,
    rs_recv,
    ag_send,
    ag_recv,
):
    n_row, n_col, n_rep, edge, chan, chunk = sizes
    n_all = n_row * n_col * n_rep
    pairs = edge // 2
    row, col, rep = lax.axis_index("row"), lax.axis_index("col"), lax.axis_index("rep")
    line = row * n_rep + rep
    n_line = n_row * n_rep
    me = line * n_col + col

    def device(index):
        across = index % n_col
        along = index // n_col
        return {"row": along // n_rep, "rep": along % n_rep, "col": across}

    barrier = pltpu.get_barrier_semaphore()
    loop(
        1,
        n_all,
        lambda d: pl.semaphore_signal(
            barrier, inc=1, device_id=device((me + d) % n_all), device_id_type=MESH
        ),
    )

    def share(ref, emb, index):
        width = emb.shape[1]
        if ref.shape[0] == width:
            return ref[...]
        return ref[pl.ds(pl.multiple_of(index * width, 16), width), :]

    keep = kept[0, 0].astype(F32)
    part_row = jnp.dot(
        emb_row[...], share(proj_row, emb_row, col), preferred_element_type=F32
    )
    part_col = jnp.dot(
        emb_col[...], share(proj_col, emb_col, row), preferred_element_type=F32
    )
    rank = part_row.shape[1]
    rowbuf[col, 8 : edge + 8, :] = part_row
    rowbuf[col, 0:8, :] = jnp.full((8, rank), keep, F32)
    rowbuf[col, edge + 8 : edge + 16, :] = jnp.full((8, rank), keep, F32)
    colbuf[row, :, :] = part_col

    pl.semaphore_wait(barrier, n_all - 1)

    def row_copy(d, src):
        return pltpu.make_async_remote_copy(
            src_ref=rowbuf.at[src],
            dst_ref=rowbuf.at[src],
            send_sem=row_send.at[d],
            recv_sem=row_recv.at[src],
            device_id={"col": (col + d) % n_col},
            device_id_type=MESH,
        )

    def redge_copy(side, d, src):
        to = (line + (1 if side == 0 else n_line - 1)) % n_line
        return pltpu.make_async_remote_copy(
            src_ref=rowbuf.at[src, pl.ds(edge if side == 0 else 0, 16)],
            dst_ref=rowedge.at[side, src],
            send_sem=redge_send.at[side, d],
            recv_sem=redge_recv.at[side, src],
            device_id={"row": to // n_rep, "rep": to % n_rep, "col": (col + d) % n_col},
            device_id_type=MESH,
        )

    def col_copy(d, src):
        return pltpu.make_async_remote_copy(
            src_ref=colbuf.at[src],
            dst_ref=colbuf.at[src],
            send_sem=col_send.at[d],
            recv_sem=col_recv.at[src],
            device_id={"row": (row + d) % n_row},
            device_id_type=MESH,
        )

    def cedge_copy(side, d, src):
        to = (col + (1 if side == 0 else n_col - 1)) % n_col
        return pltpu.make_async_remote_copy(
            src_ref=colbuf.at[src, pl.ds(edge - 8 if side == 0 else 0, 8)],
            dst_ref=coledge.at[side, src],
            send_sem=cedge_send.at[side, d],
            recv_sem=cedge_recv.at[side, src],
            device_id={"row": (row + d) % n_row, "col": to},
            device_id_type=MESH,
        )

    loop(1, n_row, lambda d: col_copy(d, row).start())
    loop(1, n_col, lambda d: row_copy(d, col).start())
    for side in range(2):
        loop(0, n_row, lambda d: cedge_copy(side, d, row).start())
        loop(0, n_col, lambda d: redge_copy(side, d, col).start())

    def widen(c, _):
        start = pl.multiple_of(c * edge, edge)
        target32[pl.ds(start, edge), :] = target[c].astype(F32)
        return 0

    lax.fori_loop(0, chan, widen, 0, unroll=4)
    for a in range(3):
        for b in range(3):
            weight_f[b * chan : (b + 1) * chan, a * chan : (a + 1) * chan] = conv_weight[
                a, b
            ].astype(F32)
    weight_t = weight_f[...].T.astype(BF16)
    out_t = pair_out[...].astype(F32).T
    pair_b = jnp.broadcast_to(pair_bias[...], (128, chan)).T
    conv_b = jnp.broadcast_to(conv_bias[...], (128, chan)).T
    zeros = jnp.zeros((2 * chan, 2 * edge), BF16)
    grad_in[0 : 2 * chan, :] = zeros
    grad_in[(pairs + 2) * chan : (pairs + 4) * chan, :] = zeros
    base[0 : 2 * chan, :] = zeros.astype(F32)
    base[(pairs + 2) * chan : (pairs + 4) * chan, :] = zeros.astype(F32)
    bias_acc[...] = jnp.zeros_like(bias_acc)
    total[...] = jnp.zeros_like(total)

    loop(1, n_row, lambda d: col_copy(d, (row + n_row - d) % n_row).wait_recv())
    loop(1, n_col, lambda d: row_copy(d, (col + n_col - d) % n_col).wait_recv())
    for side in range(2):
        loop(0, n_row, lambda d: cedge_copy(side, d, (row + n_row - d) % n_row).wait_recv())
        loop(0, n_col, lambda d: redge_copy(side, d, (col + n_col - d) % n_col).wait_recv())

    def rounded(x):
        return x.astype(BF16).astype(F32)

    row_feat[0:8, :] = rounded(sum(rowedge[0, c, 0:8, :] for c in range(n_col)))
    row_feat[8 : edge + 8, :] = rounded(sum(rowbuf[c, 8 : edge + 8, :] for c in range(n_col)))
    row_feat[edge + 8 : edge + 16, :] = rounded(
        sum(rowedge[1, c, 8:16, :] for c in range(n_col))
    )
    col_wide[0:8, :] = sum(coledge[0, r] for r in range(n_row))
    col_wide[8 : edge + 8, :] = sum(colbuf[r] for r in range(n_row))
    col_wide[edge + 8 : edge + 16, :] = sum(coledge[1, r] for r in range(n_row))
    for b in range(3):
        wide_t[b * edge : (b + 1) * edge, :] = col_wide[
            6 + 2 * b : 6 + 2 * b + edge, :
        ].astype(BF16)

    lane = lax.broadcasted_iota(jnp.int32, (1, edge), 1)
    before, after = (col + n_col - 1) % n_col, (col + 1) % n_col
    has_before = (col > 0).astype(F32)
    has_after = (col < n_col - 1).astype(F32)

    def masks(get, valid):
        here, left, right = (
            jnp.broadcast_to(get(c), (1, edge)) * scale
            for c, scale in ((col, valid), (before, valid * has_before), (after, valid * has_after))
        )
        return (jnp.where(lane < 2, left, here), here, jnp.where(lane >= edge - 2, right, here))

    top = masks(lambda c: rowedge[0, c, 8:9, 0:1], (line > 0).astype(F32))
    middle = masks(lambda c: rowbuf[c, 0:1, 0:1], jnp.float32(1))
    bottom = masks(lambda c: rowedge[1, c, 0:1, 0:1], (line < n_line - 1).astype(F32))

    def features(pair, count, mask, inner):
        scaled = []
        for r in range(2 * count):
            feat = row_feat[pl.ds(2 * pair + 8 + r, 1), :]
            scaled.append((out_t * feat).astype(BF16))
        product = lax.dot_general(
            jnp.concatenate(scaled, axis=0), wide_t[...], NT, preferred_element_type=F32
        )
        for r in range(2 * count):
            p = pair + r // 2
            lanes = slice((r % 2) * edge, (r % 2 + 1) * edge)
            for b in range(3):
                value = product[r * chan : (r + 1) * chan, b * edge : (b + 1) * edge] + pair_b
                start = pl.multiple_of((p + 1) * 3 * chan + b * chan, chan)
                hid[pl.ds(start, chan), lanes] = (jnp.maximum(value, 0.0) * mask[b]).astype(BF16)
                if inner and b == 1:
                    aim = target32[pl.ds(2 * pair + r, chan, stride=edge), :]
                    start = pl.multiple_of((p + 2) * chan, chan)
                    base[pl.ds(start, chan), lanes] = (value + conv_b) - aim

    features(-1, 1, top, False)
    features(pairs, 1, bottom, False)
    group = 4

    def feature_step(g, _):
        features(g * group, group, middle, True)
        return 0

    lax.fori_loop(0, pairs // group, feature_step, 0)

    def conv_of(p):
        start = pl.multiple_of((p + 1) * 3 * chan, 3 * chan)
        return jnp.dot(weight_t, hid[pl.ds(start, 3 * chan), :], preferred_element_type=F32)

    def slot(p):
        return pl.ds(pl.multiple_of((p + 2) * chan, chan), chan)

    def spread(p, done):
        y = conv_of(p)
        base[slot(p + 1), :] += y[0:chan]
        base[slot(p), :] += y[chan : 2 * chan]
        if done:
            differ = (base[slot(p - 1), :] + y[2 * chan :]) * keep
            grad_in[slot(p - 1), :] = differ.astype(BF16)
            bias_acc[...] += differ
            loss = 0.5 * jnp.sum(differ * differ, axis=0, keepdims=True)
            loss_out[pl.ds(2 * (p - 1), 1), :] = loss[:, 0:edge]
            loss_out[pl.ds(2 * (p - 1) + 1, 1), :] = loss[:, edge : 2 * edge]

    spread(-1, False)
    spread(0, False)

    def conv_step(g, _):
        for r in range(4):
            spread(1 + g * 4 + r, True)
        return 0

    lax.fori_loop(0, pairs // 4, conv_step, 0)

    def grad_step(g, _):
        value = total[...]
        for r in range(6):
            p = g * 6 + r - 1
            start = pl.multiple_of((p + 1) * 3 * chan, 3 * chan)
            near = pl.multiple_of((p + 1) * chan, chan)
            value = value + lax.dot_general(
                hid[pl.ds(start, 3 * chan), :],
                grad_in[pl.ds(near, 3 * chan), :],
                NT,
                preferred_element_type=F32,
            )
        total[...] = value
        return 0

    lax.fori_loop(0, (pairs + 2) // 6, grad_step, 0)

    norm = 1.0 / (edge * edge)
    half = 3 * chan // 2
    rows = 3 * chan + half
    sums = total[...] * norm
    flat = jnp.concatenate(
        [
            sums[:, 0 : 2 * chan],
            jnp.concatenate([sums[0:half, 2 * chan :], sums[half:, 2 * chan :]], axis=1),
        ],
        axis=0,
    )
    bias_sum = lax.dot_general(
        jnp.ones((8, 2 * edge), F32),
        bias_acc[...] * norm,
        NT,
        precision=lax.Precision.HIGHEST,
        preferred_element_type=F32,
    )
    part[0:rows, :] = flat
    part[rows : rows + 8, :] = jnp.concatenate([bias_sum, bias_sum], axis=1)
    rest = n_all * chunk - rows - 8
    if rest > 0:
        part[rows + 8 :, :] = jnp.zeros((rest, 128), F32)

    def piece(index):
        return pl.ds(pl.multiple_of(index * chunk, 8), chunk)

    def rs_copy(d, to, src):
        return pltpu.make_async_remote_copy(
            src_ref=part.at[piece(to)],
            dst_ref=reduced.at[src],
            send_sem=rs_send.at[d],
            recv_sem=rs_recv.at[src],
            device_id=device(to),
            device_id_type=MESH,
        )

    def ag_copy(d, to, src):
        return pltpu.make_async_remote_copy(
            src_ref=full.at[piece(src)],
            dst_ref=full.at[piece(src)],
            send_sem=ag_send.at[d],
            recv_sem=ag_recv.at[src],
            device_id=device(to),
            device_id_type=MESH,
        )

    loop(1, n_all, lambda d: rs_copy(d, (me + d) % n_all, me).start())
    reduced[me] = part[piece(me), :]
    loop(1, n_all, lambda d: rs_copy(d, (me + d) % n_all, (me + n_all - d) % n_all).wait_recv())
    if n_all <= 16:
        own = sum(reduced[r] for r in range(n_all))
    else:
        own = lax.fori_loop(
            0, n_all, lambda r, x: x + reduced[r], jnp.zeros((chunk, 128), F32)
        )
    full[piece(me), :] = own
    loop(1, n_all, lambda d: ag_copy(d, (me + d) % n_all, me).start())
    loop(1, n_all, lambda d: ag_copy(d, (me + d) % n_all, (me + n_all - d) % n_all).wait_recv())

    for b in range(3):
        low = b * chan
        conv_grad_out[2, b] = full[low : low + chan, 0:chan]
        conv_grad_out[1, b] = full[low : low + chan, chan : 2 * chan]
    low = 3 * chan
    conv_grad_out[0, 0] = full[low : low + chan, 0:chan]
    conv_grad_out[0, 1, 0 : half - chan] = full[low + chan : low + half, 0:chan]
    conv_grad_out[0, 1, half - chan :] = full[low : low + 2 * chan - half, chan : 2 * chan]
    conv_grad_out[0, 2] = full[low + 2 * chan - half : low + half, chan : 2 * chan]
    bias_out[...] = full[rows : rows + 1, 0:chan]

    loop(1, n_row, lambda d: col_copy(d, row).wait_send())
    loop(1, n_col, lambda d: row_copy(d, col).wait_send())
    for side in range(2):
        loop(0, n_row, lambda d: cedge_copy(side, d, row).wait_send())
        loop(0, n_col, lambda d: redge_copy(side, d, col).wait_send())
    loop(1, n_all, lambda d: rs_copy(d, (me + d) % n_all, me).wait_send())
    loop(1, n_all, lambda d: ag_copy(d, (me + d) % n_all, me).wait_send())


def solution(mesh):
    n_row, n_col, n_rep = (mesh.shape[axis] for axis in ("row", "col", "rep"))
    n_all = n_row * n_col * n_rep

    def per_device(
        emb_row,
        emb_col,
        proj_row,
        proj_col,
        pair_out,
        pair_bias,
        conv_weight,
        conv_bias,
        target,
        kept_tiles,
    ):
        chan, edge = target.shape[0], target.shape[1]
        rank = pair_out.shape[0]
        pairs = edge // 2
        used = 3 * chan + 3 * chan // 2 + 8
        chunk = 8 * pl.cdiv(used, 8 * n_all)

        def shared(proj, emb, axis):
            width = emb.shape[1]
            if width % 16 == 0:
                return proj
            return lax.dynamic_slice_in_dim(proj, lax.axis_index(axis) * width, width, 0)

        dma = pltpu.SemaphoreType.DMA
        vmem = pl.BlockSpec(memory_space=pltpu.VMEM)
        loss, grads, bias = pl.pallas_call(
            functools.partial(kernel, (n_row, n_col, n_rep, edge, chan, chunk)),
            out_shape=(
                jax.ShapeDtypeStruct((edge, edge), F32),
                jax.ShapeDtypeStruct((3, 3, chan, chan), F32),
                jax.ShapeDtypeStruct((1, chan), F32),
            ),
            in_specs=[vmem] * 9 + [pl.BlockSpec(memory_space=pltpu.SMEM)],
            out_specs=(vmem,) * 3,
            scratch_shapes=[
                pltpu.VMEM((n_col, edge + 16, rank), F32),
                pltpu.VMEM((2, n_col, 16, rank), F32),
                pltpu.VMEM((n_row, edge, rank), F32),
                pltpu.VMEM((2, n_row, 8, rank), F32),
                pltpu.VMEM((edge + 16, rank), F32),
                pltpu.VMEM((edge + 16, rank), F32),
                pltpu.VMEM((3 * edge, rank), BF16),
                pltpu.VMEM((chan * edge, edge), F32),
                pltpu.VMEM(((pairs + 2) * 3 * chan, 2 * edge), BF16),
                pltpu.VMEM(((pairs + 4) * chan, 2 * edge), F32),
                pltpu.VMEM(((pairs + 4) * chan, 2 * edge), BF16),
                pltpu.VMEM((3 * chan, 3 * chan), F32),
                pltpu.VMEM((3 * chan, 3 * chan), F32),
                pltpu.VMEM((chan, 2 * edge), F32),
                pltpu.VMEM((n_all * chunk, 128), F32),
                pltpu.VMEM((n_all, chunk, 128), F32),
                pltpu.VMEM((n_all * chunk, 128), F32),
                dma((n_col,)),
                dma((n_col,)),
                dma((2, n_col)),
                dma((2, n_col)),
                dma((n_row,)),
                dma((n_row,)),
                dma((2, n_row)),
                dma((2, n_row)),
                dma((n_all,)),
                dma((n_all,)),
                dma((n_all,)),
                dma((n_all,)),
            ],
            compiler_params=pltpu.CompilerParams(collective_id=0, has_side_effects=True),
            name="pair_step",
        )(
            emb_row,
            emb_col,
            shared(proj_row, emb_row, "col"),
            shared(proj_col, emb_col, "row"),
            pair_out,
            pair_bias.reshape(1, chan),
            conv_weight,
            conv_bias.reshape(1, chan),
            target,
            kept_tiles,
        )
        return loss, grads, bias.reshape(chan)

    in_specs = (
        P(("grp", "row", "rep"), "col"),
        P(("grp", "col"), "row"),
        P(),
        P(),
        P(),
        P(),
        P(),
        P(),
        P(None, ("grp", "row", "rep"), "col"),
        P(("grp", "row", "rep"), "col"),
    )
    out_specs = (P(("grp", "row", "rep"), "col"), P("grp", None, None, None), P("grp"))
    return jax.shard_map(
        per_device, mesh=mesh, in_specs=in_specs, out_specs=out_specs, check_vma=False
    )
```

profile of v0, /device:TPU:1, one launch (start us, length us, event | category | flops | bytes accessed | tf_op | source)
XLA Modules:
  0.0 54.9 jit_solution(15013415729809394333)
XLA Ops:
  1.3 1.6 %copy.13.emb_col = bf16[128,320]{1,0:T(8,128)(2,1)} copy(bf16[128,320]{0,1:T(8,128)(2,1)} %param.11) | data formatting | bytes 163840 | tf_op args[1]
  2.9 1.8 %copy.14.proj_row = bf16[1280,64]{1,0:T(8,128)(2,1)} copy(bf16[1280,64]{0,1:T(8,128)(2,1)} %param.12) | data formatting | bytes 327680 | tf_op args[2]
  4.7 1.8 %copy.15.proj_col = bf16[1280,64]{1,0:T(8,128)(2,1)} copy(bf16[1280,64]{0,1:T(8,128)(2,1)} %param.13) | data formatting | bytes 327680 | tf_op args[3]
  6.5 44.0 %pair_step.1 = (f32[128,128]{1,0:T(8,128)}, f32[3,3,64,64]{3,2,1,0:T(8,128)}, f32[1,64]{1,0:T(1,128)}) custom-call(bf16[128,640]{1,0:T(8,128)(2,1)} %emb_row.1, bf16[128,320]{1,0:T(8,128)(2,1)} %copy.13.emb_col, bf16[1280,64]{1,0:T(8,128)(2,1)} %copy.14.proj_row, bf16[1280,64]{1,0:T(8,128)(2,1)} %copy.15.proj_col, bf16[64,64]{1,0:T(8,128)(2,1)} %pair_out.1, ...), custom_call_target="tpu_custom_call" | custom-call | tf_op jit(solution)/shard_map/pair_step/pallas_call | solution.py:407
  50.5 1.5 %copy.20 = f32[128,128]{1,0:T(8,128)} copy(f32[128,128]{1,0:T(8,128)} %get-tuple-element.12) | data formatting | bytes 131072
  52.0 1.7 %copy.21 = f32[3,3,64,64]{3,2,1,0:T(8,128)} copy(f32[3,3,64,64]{3,2,1,0:T(8,128)} %get-tuple-element.13) | data formatting | bytes 294912
  53.7 1.2 %copy.22 = f32[64]{0:T(128)} copy(f32[64]{0:T(128)} %bitcast.5) | data formatting | bytes 512
where the time goes:
time: 55.3 us; the launch traced here: 54.9 us
  Pallas kernels  44 us (80%)
  local copies, waits for them, and re-layouts  9.61 us (17%)
  between operations  1.29 us (2%)
    pallas_call x1, Pallas kernels, per_device(): pl.pallas_call(functools.partial(kernel, (n_row, n_col, n_rep, edge, chan...  44 us
    unnamed x6, local copies, waits for them, and re-layouts  9.61 us

commit v1 on v0

--- a/solution.py
+++ b/solution.py
@@ -19,6 +19,20 @@
             body(d)
     else:
         lax.fori_loop(low, high, lambda d, _: (body(d), 0)[1], 0)
+
+
+def columns(ref, width, index, count):
+    everything = ref.shape[1]
+    if width % 128 == 0:
+        return ref[:, pl.ds(pl.multiple_of(index * width, 128), width)]
+    offset = max(i * width % 128 for i in range(count))
+    window = min(-(-(offset + width) // 128) * 128, everything)
+    tile = index * width // 128
+    if any(i * width // 128 * 128 + window > everything for i in range(count)):
+        tile = jnp.minimum(tile, (everything - window) // 128)
+    value = ref[:, pl.ds(pl.multiple_of(tile * 128, 128), window)].astype(F32)
+    shift = window - (index * width - tile * 128)
+    return pltpu.roll(value, shift % window, 1)[:, 0:width].astype(BF16)
 
 
 def kernel(
@@ -34,8 +48,7 @@
     target,
     kept,
     loss_out,
-    conv_grad_out,
-    bias_out,
+    full,
     rowbuf,
     rowedge,
     colbuf,
@@ -43,6 +56,7 @@
     row_feat,
     col_wide,
     wide_t,
+    target_in,
     target32,
     hid,
     base,
@@ -52,7 +66,7 @@
     bias_acc,
     part,
     reduced,
-    full,
+    target_sem,
     row_send,
     row_recv,
     redge_send,
@@ -88,19 +102,21 @@
         ),
     )
 
-    def share(ref, emb, index):
-        width = emb.shape[1]
-        if ref.shape[0] == width:
-            return ref[...]
-        return ref[pl.ds(pl.multiple_of(index * width, 16), width), :]
+    fetch = pltpu.make_async_copy(target, target_in, target_sem)
+    fetch.start()
 
     keep = kept[0, 0].astype(F32)
-    part_row = jnp.dot(
-        emb_row[...], share(proj_row, emb_row, col), preferred_element_type=F32
+    part_row = lax.dot_general(
+        emb_row[...],
+        columns(proj_row, emb_row.shape[1], col, n_col),
+        NT,
+        preferred_element_type=F32,
     )
     part_col = jnp.dot(
-        emb_col[...], share(proj_col, emb_col, row), preferred_element_type=F32
-    )
+        columns(proj_col, emb_col.shape[0], row, n_row),
+        emb_col[...],
+        preferred_element_type=F32,
+    ).T
     rank = part_row.shape[1]
     rowbuf[col, 8 : edge + 8, :] = part_row
     rowbuf[col, 0:8, :] = jnp.full((8, rank), keep, F32)
@@ -157,9 +173,11 @@
         loop(0, n_row, lambda d: cedge_copy(side, d, row).start())
         loop(0, n_col, lambda d: redge_copy(side, d, col).start())
 
+    fetch.wait()
+
     def widen(c, _):
         start = pl.multiple_of(c * edge, edge)
-        target32[pl.ds(start, edge), :] = target[c].astype(F32)
+        target32[pl.ds(start, edge), :] = target_in[c].astype(F32)
         return 0
 
     lax.fori_loop(0, chan, widen, 0, unroll=4)
@@ -354,6 +372,20 @@
     loop(1, n_all, lambda d: ag_copy(d, (me + d) % n_all, me).start())
     loop(1, n_all, lambda d: ag_copy(d, (me + d) % n_all, (me + n_all - d) % n_all).wait_recv())
 
+    loop(1, n_row, lambda d: col_copy(d, row).wait_send())
+    loop(1, n_col, lambda d: row_copy(d, col).wait_send())
+    for side in range(2):
+        loop(0, n_row, lambda d: cedge_copy(side, d, row).wait_send())
+        loop(0, n_col, lambda d: redge_copy(side, d, col).wait_send())
+    loop(1, n_all, lambda d: rs_copy(d, (me + d) % n_all, me).wait_send())
+    loop(1, n_all, lambda d: ag_copy(d, (me + d) % n_all, me).wait_send())
+
+
+def finish(loss_in, full, loss_out, conv_grad_out, bias_out):
+    chan = bias_out.shape[1]
+    half = 3 * chan // 2
+    rows = 3 * chan + half
+    loss_out[...] = loss_in[...]
     for b in range(3):
         low = b * chan
         conv_grad_out[2, b] = full[low : low + chan, 0:chan]
@@ -364,14 +396,6 @@
     conv_grad_out[0, 1, half - chan :] = full[low : low + 2 * chan - half, chan : 2 * chan]
     conv_grad_out[0, 2] = full[low + 2 * chan - half : low + half, chan : 2 * chan]
     bias_out[...] = full[rows : rows + 1, 0:chan]
-
-    loop(1, n_row, lambda d: col_copy(d, row).wait_send())
-    loop(1, n_col, lambda d: row_copy(d, col).wait_send())
-    for side in range(2):
-        loop(0, n_row, lambda d: cedge_copy(side, d, row).wait_send())
-        loop(0, n_col, lambda d: redge_copy(side, d, col).wait_send())
-    loop(1, n_all, lambda d: rs_copy(d, (me + d) % n_all, me).wait_send())
-    loop(1, n_all, lambda d: ag_copy(d, (me + d) % n_all, me).wait_send())
 
 
 def solution(mesh):
@@ -396,23 +420,17 @@
         used = 3 * chan + 3 * chan // 2 + 8
         chunk = 8 * pl.cdiv(used, 8 * n_all)
 
-        def shared(proj, emb, axis):
-            width = emb.shape[1]
-            if width % 16 == 0:
-                return proj
-            return lax.dynamic_slice_in_dim(proj, lax.axis_index(axis) * width, width, 0)
-
         dma = pltpu.SemaphoreType.DMA
         vmem = pl.BlockSpec(memory_space=pltpu.VMEM)
-        loss, grads, bias = pl.pallas_call(
+        loss, sums = pl.pallas_call(
             functools.partial(kernel, (n_row, n_col, n_rep, edge, chan, chunk)),
             out_shape=(
                 jax.ShapeDtypeStruct((edge, edge), F32),
-                jax.ShapeDtypeStruct((3, 3, chan, chan), F32),
-                jax.ShapeDtypeStruct((1, chan), F32),
+                jax.ShapeDtypeStruct((n_all * chunk, 128), F32),
             ),
-            in_specs=[vmem] * 9 + [pl.BlockSpec(memory_space=pltpu.SMEM)],
-            out_specs=(vmem,) * 3,
+            in_specs=[vmem] * 8
+            + [pl.BlockSpec(memory_space=pl.ANY), pl.BlockSpec(memory_space=pltpu.SMEM)],
+            out_specs=(vmem,) * 2,
             scratch_shapes=[
                 pltpu.VMEM((n_col, edge + 16, rank), F32),
                 pltpu.VMEM((2, n_col, 16, rank), F32),
@@ -421,6 +439,7 @@
                 pltpu.VMEM((edge + 16, rank), F32),
                 pltpu.VMEM((edge + 16, rank), F32),
                 pltpu.VMEM((3 * edge, rank), BF16),
+                pltpu.VMEM((chan, edge, edge), BF16),
                 pltpu.VMEM((chan * edge, edge), F32),
                 pltpu.VMEM(((pairs + 2) * 3 * chan, 2 * edge), BF16),
                 pltpu.VMEM(((pairs + 4) * chan, 2 * edge), F32),
@@ -430,7 +449,7 @@
                 pltpu.VMEM((chan, 2 * edge), F32),
                 pltpu.VMEM((n_all * chunk, 128), F32),
                 pltpu.VMEM((n_all, chunk, 128), F32),
-                pltpu.VMEM((n_all * chunk, 128), F32),
+                pltpu.SemaphoreType.DMA,
                 dma((n_col,)),
                 dma((n_col,)),
                 dma((2, n_col)),
@@ -448,9 +467,9 @@
             name="pair_step",
         )(
             emb_row,
-            emb_col,
-            shared(proj_row, emb_row, "col"),
-            shared(proj_col, emb_col, "row"),
+            emb_col.T,
+            proj_row.T,
+            proj_col.T,
             pair_out,
             pair_bias.reshape(1, chan),
             conv_weight,
@@ -458,6 +477,17 @@
             target,
             kept_tiles,
         )
+        loss, grads, bias = pl.pallas_call(
+            finish,
+            out_shape=(
+                jax.ShapeDtypeStruct((edge, edge), F32),
+                jax.ShapeDtypeStruct((3, 3, chan, chan), F32),
+                jax.ShapeDtypeStruct((1, chan), F32),
+            ),
+            in_specs=[vmem] * 2,
+            out_specs=(vmem,) * 3,
+            name="finish",
+        )(loss, sums)
         return loss, grads, bias.reshape(chan)
 
     in_specs = (

time: 55.3 us -> 46.4 us (0.84)
  local copies, waits for them, and re-layouts: 9.61 us -> 0 us
  Pallas kernels: 44 us -> 44.8 us
    unnamed x6 -> x0, local copies, waits for them, and re-layouts: 9.61 us -> none
    pallas_call x0 -> x1, Pallas kernels: none -> 1.79 us  [per_device(): pl.pallas_call(finish, out_shape=(jax.ShapeDtypeStruct((edge, edge), F32)...]
    pallas_call x1, Pallas kernels: 44 us -> 43 us  [per_device(): pl.pallas_call(functools.partial(kernel, (n_row, n_col, n_rep, edge, chan...]
where the time goes in v1:
time: 46.4 us; the launch traced here: 46.1 us
  Pallas kernels  44.8 us (97%)
  between operations  1.29 us (3%)
    pallas_call x1, Pallas kernels, per_device(): pl.pallas_call(functools.partial(kernel, (n_row, n_col, n_rep, edge, chan...  43 us
    pallas_call x1, Pallas kernels, per_device(): pl.pallas_call(finish, out_shape=(jax.ShapeDtypeStruct((edge, edge), F32)...  1.79 us

profile of v1, /device:TPU:1, one launch (start us, length us, event | category | flops | bytes accessed | tf_op | source)
XLA Modules:
  0.0 46.1 jit_solution(13758422989609226873)
XLA Ops:
  1.3 43.0 %pair_step.1 = (f32[128,128]{1,0:T(8,128)}, f32[384,128]{1,0:T(8,128)}) custom-call(bf16[128,640]{1,0:T(8,128)(2,1)} %emb_row.1, bf16[320,128]{1,0:T(8,128)(2,1)} %bitcast.8, bf16[64,1280]{1,0:T(8,128)(2,1)} %bitcast.6, bf16[64,1280]{1,0:T(8,128)(2,1)} %bitcast.7, bf16[64,64]{1,0:T(8,128)(2,1)} %pair_out.1, f32[1,64]{1,0:T(1,128)} %bitcast.9, ...), custom_call_target="tpu_custom_call" | custom-call | tf_op jit(solution)/shard_map/pair_step/pallas_call | solution.py:425
  44.3 1.8 %finish.1 = (f32[128,128]{1,0:T(8,128)}, f32[3,3,64,64]{3,2,1,0:T(8,128)}, f32[1,64]{1,0:T(1,128)}) custom-call(f32[128,128]{1,0:T(8,128)} %get-tuple-element.8.loss_in, f32[384,128]{1,0:T(8,128)} %get-tuple-element.9.full), custom_call_target="tpu_custom_call" | custom-call | tf_op jit(solution)/shard_map/finish/pallas_call | solution.py:480

commit v2 on v1

--- a/solution.py
+++ b/solution.py
@@ -37,18 +37,26 @@
 
 def kernel(
     sizes,
-    emb_row,
-    emb_col,
-    proj_row,
-    proj_col,
+    emb_row_hbm,
+    emb_col_hbm,
+    proj_row_hbm,
+    proj_col_hbm,
     pair_out,
     pair_bias,
-    conv_weight,
+    conv_weight_hbm,
     conv_bias,
     target,
     kept,
     loss_out,
     full,
+    emb_row,
+    emb_col,
+    proj_row,
+    proj_col,
+    conv_weight,
+    in_sem,
+    rowtail,
+    coltail,
     rowbuf,
     rowedge,
     colbuf,
@@ -102,26 +110,54 @@
         ),
     )
 
+    inputs = [
+        pltpu.make_async_copy(src, dst, in_sem.at[i])
+        for i, (src, dst) in enumerate(
+            (
+                (emb_row_hbm, emb_row),
+                (proj_row_hbm, proj_row),
+                (emb_col_hbm, emb_col),
+                (proj_col_hbm, proj_col),
+                (conv_weight_hbm, conv_weight),
+            )
+        )
+    ]
+    for copy in inputs:
+        copy.start()
     fetch = pltpu.make_async_copy(target, target_in, target_sem)
     fetch.start()
 
+    def rounded(x):
+        return x.astype(BF16).astype(F32)
+
     keep = kept[0, 0].astype(F32)
-    part_row = lax.dot_general(
-        emb_row[...],
-        columns(proj_row, emb_row.shape[1], col, n_col),
-        NT,
-        preferred_element_type=F32,
-    )
+    for copy in inputs[2:4]:
+        copy.wait()
     part_col = jnp.dot(
         columns(proj_col, emb_col.shape[0], row, n_row),
         emb_col[...],
         preferred_element_type=F32,
-    ).T
-    rank = part_row.shape[1]
-    rowbuf[col, 8 : edge + 8, :] = part_row
-    rowbuf[col, 0:8, :] = jnp.full((8, rank), keep, F32)
-    rowbuf[col, edge + 8 : edge + 16, :] = jnp.full((8, rank), keep, F32)
-    colbuf[row, :, :] = part_col
+    )
+    for copy in inputs[0:2]:
+        copy.wait()
+    part_row = lax.dot_general(
+        columns(proj_row, emb_row.shape[1], col, n_col),
+        emb_row[...],
+        NT,
+        preferred_element_type=F32,
+    )
+    rank = part_row.shape[0]
+    colbuf[row] = part_col.astype(BF16)
+    rowbuf[col, 0:rank, :] = part_row.astype(BF16)
+    rowbuf[col, rank:, :] = jnp.full((16, edge), keep, F32).astype(BF16)
+    turned = rounded(part_col).T
+    coltail[0] = turned[edge - 8 :]
+    coltail[1] = turned[0:8]
+    turned = rounded(part_row).T
+    rowtail[0, 0:8] = turned[edge - 8 :]
+    rowtail[1, 0:8] = turned[0:8]
+    for side in range(2):
+        rowtail[side, 8:16] = jnp.full((8, rank), keep, F32)
 
     pl.semaphore_wait(barrier, n_all - 1)
 
@@ -138,7 +174,7 @@
     def redge_copy(side, d, src):
         to = (line + (1 if side == 0 else n_line - 1)) % n_line
         return pltpu.make_async_remote_copy(
-            src_ref=rowbuf.at[src, pl.ds(edge if side == 0 else 0, 16)],
+            src_ref=rowtail.at[side],
             dst_ref=rowedge.at[side, src],
             send_sem=redge_send.at[side, d],
             recv_sem=redge_recv.at[side, src],
@@ -159,7 +195,7 @@
     def cedge_copy(side, d, src):
         to = (col + (1 if side == 0 else n_col - 1)) % n_col
         return pltpu.make_async_remote_copy(
-            src_ref=colbuf.at[src, pl.ds(edge - 8 if side == 0 else 0, 8)],
+            src_ref=coltail.at[side],
             dst_ref=coledge.at[side, src],
             send_sem=cedge_send.at[side, d],
             recv_sem=cedge_recv.at[side, src],
@@ -174,6 +210,7 @@
         loop(0, n_col, lambda d: redge_copy(side, d, col).start())
 
     fetch.wait()
+    inputs[4].wait()
 
     def widen(c, _):
         start = pl.multiple_of(c * edge, edge)
@@ -204,17 +241,15 @@
         loop(0, n_row, lambda d: cedge_copy(side, d, (row + n_row - d) % n_row).wait_recv())
         loop(0, n_col, lambda d: redge_copy(side, d, (col + n_col - d) % n_col).wait_recv())
 
-    def rounded(x):
-        return x.astype(BF16).astype(F32)
-
-    row_feat[0:8, :] = rounded(sum(rowedge[0, c, 0:8, :] for c in range(n_col)))
-    row_feat[8 : edge + 8, :] = rounded(sum(rowbuf[c, 8 : edge + 8, :] for c in range(n_col)))
-    row_feat[edge + 8 : edge + 16, :] = rounded(
-        sum(rowedge[1, c, 8:16, :] for c in range(n_col))
-    )
-    col_wide[0:8, :] = sum(coledge[0, r] for r in range(n_row))
-    col_wide[8 : edge + 8, :] = sum(colbuf[r] for r in range(n_row))
-    col_wide[edge + 8 : edge + 16, :] = sum(coledge[1, r] for r in range(n_row))
+    def summed(terms):
+        return sum(x.astype(F32) for x in terms)
+
+    row_feat[0:8, :] = rounded(summed(rowedge[0, c, 0:8, :] for c in range(n_col)))
+    row_feat[8 : edge + 8, :] = rounded(summed(rowbuf[c, 0:rank, :] for c in range(n_col))).T
+    row_feat[edge + 8 :, :] = rounded(summed(rowedge[1, c, 0:8, :] for c in range(n_col)))
+    col_wide[0:8, :] = summed(coledge[0, r] for r in range(n_row))
+    col_wide[8 : edge + 8, :] = summed(colbuf[r] for r in range(n_row)).T
+    col_wide[edge + 8 :, :] = summed(coledge[1, r] for r in range(n_row))
     for b in range(3):
         wide_t[b * edge : (b + 1) * edge, :] = col_wide[
             6 + 2 * b : 6 + 2 * b + edge, :
@@ -233,8 +268,8 @@
         return (jnp.where(lane < 2, left, here), here, jnp.where(lane >= edge - 2, right, here))
 
     top = masks(lambda c: rowedge[0, c, 8:9, 0:1], (line > 0).astype(F32))
-    middle = masks(lambda c: rowbuf[c, 0:1, 0:1], jnp.float32(1))
-    bottom = masks(lambda c: rowedge[1, c, 0:1, 0:1], (line < n_line - 1).astype(F32))
+    middle = masks(lambda c: rowbuf[c, rank:, 0:1].astype(F32)[0:1], jnp.float32(1))
+    bottom = masks(lambda c: rowedge[1, c, 8:9, 0:1], (line < n_line - 1).astype(F32))
 
     def features(pair, count, mask, inner):
         scaled = []
@@ -351,8 +386,8 @@
 
     def ag_copy(d, to, src):
         return pltpu.make_async_remote_copy(
-            src_ref=full.at[piece(src)],
-            dst_ref=full.at[piece(src)],
+            src_ref=full.at[src],
+            dst_ref=full.at[src],
             send_sem=ag_send.at[d],
             recv_sem=ag_recv.at[src],
             device_id=device(to),
@@ -368,7 +403,7 @@
         own = lax.fori_loop(
             0, n_all, lambda r, x: x + reduced[r], jnp.zeros((chunk, 128), F32)
         )
-    full[piece(me), :] = own
+    full[me] = own.astype(BF16)
     loop(1, n_all, lambda d: ag_copy(d, (me + d) % n_all, me).start())
     loop(1, n_all, lambda d: ag_copy(d, (me + d) % n_all, (me + n_all - d) % n_all).wait_recv())
 
@@ -381,7 +416,13 @@
     loop(1, n_all, lambda d: ag_copy(d, (me + d) % n_all, me).wait_send())
 
 
-def finish(loss_in, full, loss_out, conv_grad_out, bias_out):
+def finish(loss_in, gathered, loss_out, conv_grad_out, bias_out, full):
+    n_all, chunk = gathered.shape[0:2]
+
+    def place(r):
+        full[pl.ds(r * chunk, chunk), :] = gathered[r].astype(F32)
+
+    loop(0, n_all, place)
     chan = bias_out.shape[1]
     half = 3 * chan // 2
     rows = 3 * chan + half
@@ -422,19 +463,29 @@
 
         dma = pltpu.SemaphoreType.DMA
         vmem = pl.BlockSpec(memory_space=pltpu.VMEM)
+        hbm = pl.BlockSpec(memory_space=pl.ANY)
         loss, sums = pl.pallas_call(
             functools.partial(kernel, (n_row, n_col, n_rep, edge, chan, chunk)),
             out_shape=(
                 jax.ShapeDtypeStruct((edge, edge), F32),
-                jax.ShapeDtypeStruct((n_all * chunk, 128), F32),
+                jax.ShapeDtypeStruct((n_all, chunk, 128), BF16),
             ),
-            in_specs=[vmem] * 8
-            + [pl.BlockSpec(memory_space=pl.ANY), pl.BlockSpec(memory_space=pltpu.SMEM)],
+            in_specs=[hbm] * 4
+            + [vmem] * 2
+            + [hbm, vmem, hbm, pl.BlockSpec(memory_space=pltpu.SMEM)],
             out_specs=(vmem,) * 2,
             scratch_shapes=[
-                pltpu.VMEM((n_col, edge + 16, rank), F32),
+                pltpu.VMEM(emb_row.shape, BF16),
+                pltpu.VMEM(emb_col.shape[::-1], BF16),
+                pltpu.VMEM(proj_row.shape[::-1], BF16),
+                pltpu.VMEM(proj_col.shape[::-1], BF16),
+                pltpu.VMEM(conv_weight.shape, BF16),
+                dma((5,)),
+                pltpu.VMEM((2, 16, rank), F32),
+                pltpu.VMEM((2, 8, rank), F32),
+                pltpu.VMEM((n_col, rank + 16, edge), BF16),
                 pltpu.VMEM((2, n_col, 16, rank), F32),
-                pltpu.VMEM((n_row, edge, rank), F32),
+                pltpu.VMEM((n_row, rank, edge), BF16),
                 pltpu.VMEM((2, n_row, 8, rank), F32),
                 pltpu.VMEM((edge + 16, rank), F32),
                 pltpu.VMEM((edge + 16, rank), F32),
@@ -486,6 +537,7 @@
             ),
             in_specs=[vmem] * 2,
             out_specs=(vmem,) * 3,
+            scratch_shapes=[pltpu.VMEM((n_all * chunk, 128), F32)],
             name="finish",
         )(loss, sums)
         return loss, grads, bias.reshape(chan)

time: 46.4 us -> 42 us (0.905)
  Pallas kernels: 44.8 us -> 40.1 us
    pallas_call x1, Pallas kernels: 43 us -> 38.3 us  [per_device(): pl.pallas_call(functools.partial(kernel, (n_row, n_col, n_rep, edge, chan...]
where the time goes in v2:
time: 42 us; the launch traced here: 41.3 us
  Pallas kernels  40.1 us (95%)
  between operations  1.29 us (3%)
    pallas_call x1, Pallas kernels, per_device(): pl.pallas_call(functools.partial(kernel, (n_row, n_col, n_rep, edge, chan...  38.3 us
    pallas_call x1, Pallas kernels, per_device(): pl.pallas_call(finish, out_shape=(jax.ShapeDtypeStruct((edge, edge), F32)...  1.75 us

profile of v2, /device:TPU:1, one launch (start us, length us, event | category | flops | bytes accessed | tf_op | source)
XLA Modules:
  0.0 41.3 jit_solution(81742200833594992)
XLA Ops:
  1.3 38.3 %pair_step.1 = (f32[128,128]{1,0:T(8,128)}, bf16[16,24,128]{2,1,0:T(8,128)(2,1)}) custom-call(bf16[128,640]{1,0:T(8,128)(2,1)} %emb_row_hbm.1, bf16[320,128]{1,0:T(8,128)(2,1)} %bitcast.8, bf16[64,1280]{1,0:T(8,128)(2,1)} %bitcast.6, bf16[64,1280]{1,0:T(8,128)(2,1)} %bitcast.7, bf16[64,64]{1,0:T(8,128)(2,1)} %pair_out.1, f32[1,64]{1,0:T(1,128)} %bitcast.9, ...), custom_call_target="tpu_custom_call" | custom-call | tf_op jit(solution)/shard_map/pair_step/pallas_call | solution.py:467
  39.6 1.8 %finish.1 = (f32[128,128]{1,0:T(8,128)}, f32[3,3,64,64]{3,2,1,0:T(8,128)}, f32[1,64]{1,0:T(1,128)}) custom-call(f32[128,128]{1,0:T(8,128)} %get-tuple-element.8.loss_in, bf16[16,24,128]{2,1,0:T(8,128)(2,1)} %get-tuple-element.9.gathered), custom_call_target="tpu_custom_call" | custom-call | tf_op jit(solution)/shard_map/finish/pallas_call | solution.py:531

commit v3 on v2

--- a/solution.py
+++ b/solution.py
@@ -295,12 +295,6 @@
     features(pairs, 1, bottom, False)
     group = 4
 
-    def feature_step(g, _):
-        features(g * group, group, middle, True)
-        return 0
-
-    lax.fori_loop(0, pairs // group, feature_step, 0)
-
     def conv_of(p):
         start = pl.multiple_of((p + 1) * 3 * chan, 3 * chan)
         return jnp.dot(weight_t, hid[pl.ds(start, 3 * chan), :], preferred_element_type=F32)
@@ -320,20 +314,10 @@
             loss_out[pl.ds(2 * (p - 1), 1), :] = loss[:, 0:edge]
             loss_out[pl.ds(2 * (p - 1) + 1, 1), :] = loss[:, edge : 2 * edge]
 
-    spread(-1, False)
-    spread(0, False)
-
-    def conv_step(g, _):
-        for r in range(4):
-            spread(1 + g * 4 + r, True)
-        return 0
-
-    lax.fori_loop(0, pairs // 4, conv_step, 0)
-
-    def grad_step(g, _):
+    def grads(first, count):
         value = total[...]
-        for r in range(6):
-            p = g * 6 + r - 1
+        for r in range(count):
+            p = first + r
             start = pl.multiple_of((p + 1) * 3 * chan, 3 * chan)
             near = pl.multiple_of((p + 1) * chan, chan)
             value = value + lax.dot_general(
@@ -343,9 +327,36 @@
                 preferred_element_type=F32,
             )
         total[...] = value
+
+    for g in range(3):
+        features(g * group, group, middle, True)
+    spread(-1, False)
+    spread(0, False)
+    for r in range(group):
+        spread(1 + r, True)
+    lag = 2 * group - 1
+
+    def step(g, _):
+        grads(g * group - 3 * group - 1, group)
+        for r in range(group):
+            spread(g * group - lag + r, True)
+        features(g * group, group, middle, True)
         return 0
 
-    lax.fori_loop(0, (pairs + 2) // 6, grad_step, 0)
+    lax.fori_loop(3, pairs // group, step, 0)
+
+    def conv_step(g, _):
+        for r in range(group):
+            spread(pairs - lag + g * group + r, True)
+        return 0
+
+    lax.fori_loop(0, 2, conv_step, 0)
+
+    def grad_step(g, _):
+        grads(pairs - 3 * group - 1 + g * 7, 7)
+        return 0
+
+    lax.fori_loop(0, 2, grad_step, 0)
 
     norm = 1.0 / (edge * edge)
     half = 3 * chan // 2
@@ -403,7 +414,7 @@
         own = lax.fori_loop(
             0, n_all, lambda r, x: x + reduced[r], jnp.zeros((chunk, 128), F32)
         )
-    full[me] = own.astype(BF16)
+    full[me] = own
     loop(1, n_all, lambda d: ag_copy(d, (me + d) % n_all, me).start())
     loop(1, n_all, lambda d: ag_copy(d, (me + d) % n_all, (me + n_all - d) % n_all).wait_recv())
 
@@ -420,7 +431,7 @@
     n_all, chunk = gathered.shape[0:2]
 
     def place(r):
-        full[pl.ds(r * chunk, chunk), :] = gathered[r].astype(F32)
+        full[pl.ds(r * chunk, chunk), :] = gathered[r]
 
     loop(0, n_all, place)
     chan = bias_out.shape[1]
@@ -468,7 +479,7 @@
             functools.partial(kernel, (n_row, n_col, n_rep, edge, chan, chunk)),
             out_shape=(
                 jax.ShapeDtypeStruct((edge, edge), F32),
-                jax.ShapeDtypeStruct((n_all, chunk, 128), BF16),
+                jax.ShapeDtypeStruct((n_all, chunk, 128), F32),
             ),
             in_specs=[hbm] * 4
             + [vmem] * 2

time: 42 us -> 39.7 us (0.945)
  Pallas kernels: 40.1 us -> 38.2 us
    pallas_call x1, Pallas kernels: 38.3 us -> 36.4 us  [per_device(): pl.pallas_call(functools.partial(kernel, (n_row, n_col, n_rep, edge, chan...]
where the time goes in v3:
time: 39.7 us; the launch traced here: 39.4 us
  Pallas kernels  38.2 us (96%)
  between operations  1.29 us (3%)
    pallas_call x1, Pallas kernels, per_device(): pl.pallas_call(functools.partial(kernel, (n_row, n_col, n_rep, edge, chan...  36.4 us
    pallas_call x1, Pallas kernels, per_device(): pl.pallas_call(finish, out_shape=(jax.ShapeDtypeStruct((edge, edge), F32)...  1.79 us

profile of v3, /device:TPU:1, one launch (start us, length us, event | category | flops | bytes accessed | tf_op | source)
XLA Modules:
  0.0 39.4 jit_solution(3815731676029167618)
XLA Ops:
  1.3 36.4 %pair_step.1 = (f32[128,128]{1,0:T(8,128)}, f32[16,24,128]{2,1,0:T(8,128)}) custom-call(bf16[128,640]{1,0:T(8,128)(2,1)} %emb_row_hbm.1, bf16[320,128]{1,0:T(8,128)(2,1)} %bitcast.8, bf16[64,1280]{1,0:T(8,128)(2,1)} %bitcast.6, bf16[64,1280]{1,0:T(8,128)(2,1)} %bitcast.7, bf16[64,64]{1,0:T(8,128)(2,1)} %pair_out.1, f32[1,64]{1,0:T(1,128)} %bitcast.9, ...), custom_call_target="tpu_custom_call" | custom-call | tf_op jit(solution)/shard_map/pair_step/pallas_call | solution.py:478
  37.7 1.8 %finish.1 = (f32[128,128]{1,0:T(8,128)}, f32[3,3,64,64]{3,2,1,0:T(8,128)}, f32[1,64]{1,0:T(1,128)}) custom-call(f32[128,128]{1,0:T(8,128)} %get-tuple-element.8.loss_in, f32[16,24,128]{2,1,0:T(8,128)} %get-tuple-element.9.gathered), custom_call_target="tpu_custom_call" | custom-call | tf_op jit(solution)/shard_map/finish/pallas_call | solution.py:542

commit v4 on v3

--- a/solution.py
+++ b/solution.py
@@ -147,13 +147,13 @@
         preferred_element_type=F32,
     )
     rank = part_row.shape[0]
-    colbuf[row] = part_col.astype(BF16)
-    rowbuf[col, 0:rank, :] = part_row.astype(BF16)
-    rowbuf[col, rank:, :] = jnp.full((16, edge), keep, F32).astype(BF16)
-    turned = rounded(part_col).T
+    colbuf[row] = part_col
+    rowbuf[col, 0:rank, :] = part_row
+    rowbuf[col, rank:, :] = jnp.full((8, edge), keep, F32)
+    turned = part_col.T
     coltail[0] = turned[edge - 8 :]
     coltail[1] = turned[0:8]
-    turned = rounded(part_row).T
+    turned = part_row.T
     rowtail[0, 0:8] = turned[edge - 8 :]
     rowtail[1, 0:8] = turned[0:8]
     for side in range(2):
@@ -242,7 +242,7 @@
         loop(0, n_col, lambda d: redge_copy(side, d, (col + n_col - d) % n_col).wait_recv())
 
     def summed(terms):
-        return sum(x.astype(F32) for x in terms)
+        return sum(terms)
 
     row_feat[0:8, :] = rounded(summed(rowedge[0, c, 0:8, :] for c in range(n_col)))
     row_feat[8 : edge + 8, :] = rounded(summed(rowbuf[c, 0:rank, :] for c in range(n_col))).T
@@ -268,7 +268,7 @@
         return (jnp.where(lane < 2, left, here), here, jnp.where(lane >= edge - 2, right, here))
 
     top = masks(lambda c: rowedge[0, c, 8:9, 0:1], (line > 0).astype(F32))
-    middle = masks(lambda c: rowbuf[c, rank:, 0:1].astype(F32)[0:1], jnp.float32(1))
+    middle = masks(lambda c: rowbuf[c, rank : rank + 1, 0:1], jnp.float32(1))
     bottom = masks(lambda c: rowedge[1, c, 8:9, 0:1], (line < n_line - 1).astype(F32))
 
     def features(pair, count, mask, inner):
@@ -494,9 +494,9 @@
                 dma((5,)),
                 pltpu.VMEM((2, 16, rank), F32),
                 pltpu.VMEM((2, 8, rank), F32),
-                pltpu.VMEM((n_col, rank + 16, edge), BF16),
+                pltpu.VMEM((n_col, rank + 8, edge), F32),
                 pltpu.VMEM((2, n_col, 16, rank), F32),
-                pltpu.VMEM((n_row, rank, edge), BF16),
+                pltpu.VMEM((n_row, rank, edge), F32),
                 pltpu.VMEM((2, n_row, 8, rank), F32),
                 pltpu.VMEM((edge + 16, rank), F32),
                 pltpu.VMEM((edge + 16, rank), F32),

time: 39.7 us -> 40.8 us (1.028)
  Pallas kernels: 38.2 us -> 39.3 us
    pallas_call x1, Pallas kernels: 36.4 us -> 37.5 us  [per_device(): pl.pallas_call(functools.partial(kernel, (n_row, n_col, n_rep, edge, chan...]
where the time goes in v4:
time: 40.8 us; the launch traced here: 40.5 us
  Pallas kernels  39.3 us (96%)
  between operations  1.29 us (3%)
    pallas_call x1, Pallas kernels, per_device(): pl.pallas_call(functools.partial(kernel, (n_row, n_col, n_rep, edge, chan...  37.5 us
    pallas_call x1, Pallas kernels, per_device(): pl.pallas_call(finish, out_shape=(jax.ShapeDtypeStruct((edge, edge), F32)...  1.79 us

profile of v4, /device:TPU:1, one launch (start us, length us, event | category | flops | bytes accessed | tf_op | source)
XLA Modules:
  0.0 40.5 jit_solution(13365375002521963296)
XLA Ops:
  1.3 37.5 %pair_step.1 = (f32[128,128]{1,0:T(8,128)}, f32[16,24,128]{2,1,0:T(8,128)}) custom-call(bf16[128,640]{1,0:T(8,128)(2,1)} %emb_row_hbm.1, bf16[320,128]{1,0:T(8,128)(2,1)} %bitcast.8, bf16[64,1280]{1,0:T(8,128)(2,1)} %bitcast.6, bf16[64,1280]{1,0:T(8,128)(2,1)} %bitcast.7, bf16[64,64]{1,0:T(8,128)(2,1)} %pair_out.1, f32[1,64]{1,0:T(1,128)} %bitcast.9, ...), custom_call_target="tpu_custom_call" | custom-call | tf_op jit(solution)/shard_map/pair_step/pallas_call | solution.py:478
  38.8 1.8 %finish.1 = (f32[128,128]{1,0:T(8,128)}, f32[3,3,64,64]{3,2,1,0:T(8,128)}, f32[1,64]{1,0:T(1,128)}) custom-call(f32[128,128]{1,0:T(8,128)} %get-tuple-element.8.loss_in, f32[16,24,128]{2,1,0:T(8,128)} %get-tuple-element.9.gathered), custom_call_target="tpu_custom_call" | custom-call | tf_op jit(solution)/shard_map/finish/pallas_call | solution.py:542
